TPU v7x, 512 devices: a whole 4x8x8 slice. The times are simulated.
512 devices in a mesh: pts: 64 (over z, y), freq: 8 (over x, core).
Axes of the slice: x: 4, y: 8, z: 8, core: 2. Of those that a mesh axis runs over, the one named last changes fastest.
Arguments:
- snapshots: float32 [2112, 196608], P(None, ('pts', 'freq')), may hold values from -6 to 6
- weight: float32 [196608], P('pts'), may hold values from 0.1 to 10
- start_vec: float32 [64, 2, 32], replicated, may hold values from -6 to 6
Outputs:
- gram_mine: float32 [64, 2, 32, 32], P('freq')
- modes: float32 [64, 2, 196608], P('freq', None, 'pts')
All inputs are finite; a program needn't handle non-finite values.
Results may differ from a plain program's by a relative error of at most 0.0003.
Values sent between devices are 32-bit elements; how exact they have to be, the bound alone decides.
A program may use at most 64 MiB of HBM per device.

v0:
```python
import functools
import math

import jax
import jax.numpy as jnp
import numpy as np
from jax import lax
from jax.experimental import pallas as pl
from jax.experimental.pallas import tpu as pltpu
from jax.sharding import PartitionSpec as P

NFFT = 128
NB = 32
NF = 64
HALF = NFFT // 2
NC = 8
NY = 8
MESH = pl.DeviceIdType.MESH
BF = jnp.bfloat16
F32 = jnp.float32


def dft_operand():
    times = np.arange(NFFT)
    phases = (np.arange(NF)[:, None] * times[None, :] % NFFT) * (2.0 * math.pi / NFFT)
    window = 0.5 - 0.5 * np.cos(times * (2.0 * math.pi / NFFT))
    window = window / np.sqrt(np.sum(window * window))
    rows = np.stack([np.cos(phases) * window, -np.sin(phases) * window], axis=1)
    rows = rows.reshape(2 * NF, NFFT).astype(np.float32)
    high = rows.astype(BF)
    low = (rows - high.astype(np.float32)).astype(BF)
    zero = np.zeros_like(low[:, :HALF])
    top = np.concatenate([high[:, :HALF], high[:, :HALF], high[:, HALF:], high[:, HALF:]], axis=1)
    bottom = np.concatenate([low[:, :HALF], zero, low[:, HALF:], zero], axis=1)
    return np.concatenate([top, bottom], axis=0)


def split(value):
    high = value.astype(BF)
    return high, (value - high.astype(F32)).astype(BF)


def dot(a, b):
    return lax.dot_general(a, b, (((1,), (0,)), ((), ())), preferred_element_type=F32)


def dot_t(a, b):
    return lax.dot_general(a, b, (((1,), (1,)), ((), ())), preferred_element_type=F32)


def lanes(shape, axis=1):
    return lax.broadcasted_iota(jnp.int32, shape, axis)


def kernel(
    nz,
    total_rows,
    snap_hbm,
    weight_ref,
    start_ref,
    table_ref,
    gram_out,
    modes_out,
    x_ref,
    xc_ref,
    q_ref,
    ah_ref,
    al_ref,
    gs_ref,
    gr_ref,
    gx_ref,
    gy_ref,
    gz_ref,
    gf_ref,
    vy_ref,
    vz_ref,
    e_ref,
    ms_ref,
    mr_ref,
    sa_ref,
    sb_ref,
    load_sem,
    gx_s,
    gx_r,
    gy_s,
    gy_r,
    gz_s,
    gz_r,
    ga_s,
    ga_r,
    vy_s,
    vy_r,
    vz_s,
    vz_r,
    e_s,
    e_r,
    m_s,
    m_r,
):
    halves = x_ref.shape[0] // HALF
    rows = x_ref.shape[1]
    pts = lax.axis_index("pts")
    me = lax.axis_index("freq")
    zc = pts // NY
    yc = pts % NY
    xc = me // 2
    core = me % 2

    chunks = load_sem.shape[0]
    span = x_ref.shape[0] // chunks

    def load(i):
        part = pl.ds(i * span, span)
        return pltpu.make_async_copy(snap_hbm.at[part, :], x_ref.at[part, :], load_sem.at[i])

    for i in range(chunks):
        load(i).start()

    def freq_peer(i):
        return ((xc + 3 - i // 2) % (NC // 2)) * 2 + (core + 1 - i % 2) % 2

    barrier = pltpu.get_barrier_semaphore()
    for i in range(NC - 1):
        pl.semaphore_signal(barrier, inc=1, device_id={"freq": freq_peer(i)}, device_id_type=MESH)
    for d in range(1, NY):
        pl.semaphore_signal(
            barrier, inc=1, device_id={"pts": zc * NY + (yc + d) % NY}, device_id_type=MESH
        )
    for d in range(1, nz):
        pl.semaphore_signal(
            barrier, inc=1, device_id={"pts": (zc + d) % nz * NY + yc}, device_id_type=MESH
        )

    groups = rows // 128
    weight = jnp.concatenate(
        [weight_ref[pl.ds(me * groups + j, 1), :] for j in range(groups)], axis=1
    )
    root = jnp.sqrt(weight)
    inv_root = 1.0 / root
    eye = lanes((NB, NB), 0) == lanes((NB, NB), 1)

    def column(k, c):
        row = start_ref[me * (NF // NC) + k, pl.ds(c, 1), :]
        col = jnp.sum(jnp.where(eye, row, 0.0), axis=1, keepdims=True)
        return jnp.broadcast_to(col, (NB, 128))

    seg = lanes((NB, 128)) // 32
    for p in range(NF // NC // 2):
        r1, i1 = column(2 * p, 0), column(2 * p, 1)
        r2, i2 = column(2 * p + 1, 0), column(2 * p + 1, 1)
        sa_ref[p] = jnp.where(seg == 0, r1, jnp.where(seg == 1, r2, jnp.where(seg == 2, i1, i2)))
        sb_ref[p] = jnp.where(seg == 0, i1, jnp.where(seg == 1, i2, jnp.where(seg == 2, -r1, -r2)))

    total = jnp.zeros((24, rows), F32)
    for i in range(chunks):
        load(i).wait()
        for j in range(span // 24):
            total = total + x_ref[i * span + j * 24 : i * span + (j + 1) * 24, :]
    mean = jnp.sum(total, axis=0, keepdims=True) * (1.0 / x_ref.shape[0])

    def centre(j):
        high, low = split(x_ref[pl.ds(pl.multiple_of(j * HALF, HALF), HALF), :] - mean)
        xc_ref[pl.ds(pl.multiple_of(j * NFFT, NFFT), HALF), :] = high
        xc_ref[pl.ds(pl.multiple_of(j * NFFT + HALF, HALF), HALF), :] = low

    centre(0)
    centre(1)

    def transform(b, carry):
        both = dot(table_ref[...], xc_ref[pl.ds(pl.multiple_of(b * NFFT, NFFT), 2 * NFFT), :])
        value = (both[: 2 * NF] + both[2 * NF :]) * root
        for j in range(groups):
            q_ref[j, pl.ds(b, 2 * NF, stride=NB), :] = value[:, j * 128 : (j + 1) * 128]
        centre(jnp.minimum(b + 2, halves - 1))
        return carry

    lax.fori_loop(0, NB, transform, 0)

    pl.semaphore_wait(barrier, NC - 1 + NY - 1 + nz - 1)

    per = NF // NC
    block = per * 2 * NB

    def gram_copy(to, slot):
        return pltpu.make_async_remote_copy(
            src_ref=gs_ref.at[to],
            dst_ref=gr_ref.at[slot],
            send_sem=gx_s.at[to],
            recv_sem=gx_r.at[slot],
            device_id={"freq": to},
            device_id_type=MESH,
        )

    def gram_of(owner):
        for p in range(per // 2):
            first = pl.multiple_of(owner * block + p * 128, 128)
            value = [q_ref[j, pl.ds(first, 128), :] for j in range(groups)]
            high, low = split(jnp.concatenate(value, axis=1))
            ah_ref[pl.ds(first, 128), :] = high
            al_ref[pl.ds(first, 128), :] = low

            def reim(v):
                return (
                    jnp.concatenate([v[0:32], v[64:96]], axis=0),
                    jnp.concatenate([v[32:64], v[96:128]], axis=0),
                )

            rh, ih = reim(high)
            rl, il = reim(low)
            h1 = jnp.concatenate([rh, ih], axis=1)
            l1 = jnp.concatenate([rl, il], axis=1)
            h2 = jnp.concatenate([ih, -rh], axis=1)
            l2 = jnp.concatenate([il, -rl], axis=1)
            out = dot_t(
                jnp.concatenate([h1, l1], axis=0), jnp.concatenate([h1, h2, l1, l2], axis=0)
            )
            z = out[0:64, 0:128] + (out[0:64, 128:256] + out[64:128, 0:128])
            gs_ref[owner, pl.ds(p * NB, NB), :] = jnp.where(seg % 2 == 0, z[0:32], z[32:64])

    def gram_step(i, carry):
        owner = freq_peer(i)
        gram_of(owner)
        gram_copy(owner, me).start()
        return carry

    lax.fori_loop(0, NC - 1, gram_step, 0)
    gram_of(me)

    gx_ref[...] = gs_ref[me]

    def gram_sum(i, carry):
        sender = ((xc + 1 + i // 2) % (NC // 2)) * 2 + (core + 1 - i % 2) % 2
        gram_copy(sender, sender).wait_recv()
        gx_ref[...] += gr_ref[sender]
        return carry

    lax.fori_loop(0, NC - 1, gram_sum, 0)

    parts_a, parts_b = [], []
    for p in range(per // 2):
        g = gx_ref[p * NB : (p + 1) * NB, :]
        parts_a.append(jnp.sum(g * sa_ref[p], axis=0, keepdims=True))
        parts_b.append(jnp.sum(g * sb_ref[p], axis=0, keepdims=True))
    vy_ref[yc] = jnp.concatenate(parts_a + parts_b, axis=0)

    gsub = gx_ref.shape[0] // NY

    def y_dev(other):
        return {"pts": zc * NY + other}

    def z_dev(other):
        return {"pts": other * NY + yc}

    def spread(buf, ssem, rsem, mine, other, device):
        return pltpu.make_async_remote_copy(
            src_ref=buf.at[mine],
            dst_ref=buf.at[mine],
            send_sem=ssem.at[other],
            recv_sem=rsem.at[mine],
            device_id=device,
            device_id_type=MESH,
        )

    def arrival(buf, ssem, rsem, other, device):
        return pltpu.make_async_remote_copy(
            src_ref=buf.at[other],
            dst_ref=buf.at[other],
            send_sem=ssem.at[other],
            recv_sem=rsem.at[other],
            device_id=device,
            device_id_type=MESH,
        )

    def total_of(buf, n):
        out = buf[0]
        for i in range(1, n):
            out = out + buf[i]
        return out

    for d in range(1, NY):
        other = (yc + d) % NY
        spread(vy_ref, vy_s, vy_r, yc, other, y_dev(other)).start()

    def gram_y(other, slot):
        return pltpu.make_async_remote_copy(
            src_ref=gx_ref.at[pl.ds(pl.multiple_of(other * gsub, gsub), gsub), :],
            dst_ref=gy_ref.at[slot],
            send_sem=gy_s.at[other],
            recv_sem=gy_r.at[slot],
            device_id=y_dev(other),
            device_id_type=MESH,
        )

    for d in range(1, NY):
        gram_y((yc + d) % NY, yc).start()
    gy_ref[yc] = gx_ref[pl.ds(pl.multiple_of(yc * gsub, gsub), gsub), :]

    for d in range(1, NY):
        other = (yc + d) % NY
        arrival(vy_ref, vy_s, vy_r, other, y_dev(other)).wait_recv()
    vz_ref[zc] = total_of(vy_ref, NY)
    for d in range(1, nz):
        other = (zc + d) % nz
        spread(vz_ref, vz_s, vz_r, zc, other, z_dev(other)).start()

    for d in range(1, NY):
        other = (yc + d) % NY
        gram_y(other, other).wait_recv()
    gz_ref[zc] = total_of(gy_ref, NY)
    for d in range(1, nz):
        other = (zc + d) % nz
        spread(gz_ref, gz_s, gz_r, zc, other, z_dev(other)).start()

    for d in range(1, nz):
        other = (zc + d) % nz
        arrival(vz_ref, vz_s, vz_r, other, z_dev(other)).wait_recv()
    v = total_of(vz_ref, nz) * (1.0 / total_rows)

    lane = lanes((per // 2, 128))
    odd = (lane // 32) % 2 == 1
    va, vb = v[0 : per // 2], v[per // 2 :]
    vr = va + pltpu.roll(va, 64, 1)
    vi = vb + pltpu.roll(vb, 64, 1)
    square = vr * vr + vi * vi
    norm1 = jnp.sum(jnp.where(lane < 32, square, 0.0), axis=1, keepdims=True) * (1.0 / NB)
    norm2 = jnp.sum(jnp.where((lane >= 32) & (lane < 64), square, 0.0), axis=1, keepdims=True)
    norm2 = norm2 * (1.0 / NB)
    scale = jnp.where(odd, 1.0 / jnp.sqrt(norm2 + 1e-06), 1.0 / jnp.sqrt(norm1 + 1e-06))
    yr = vr * scale
    yi = vi * scale
    k1re = jnp.where(odd, -pltpu.roll(yi, 32, 1), yr)
    k1im = jnp.where(odd, pltpu.roll(yr, 32, 1), yi)
    k2re = jnp.where(odd, -yi, pltpu.roll(yr, 96, 1))
    k2im = jnp.where(odd, yr, pltpu.roll(yi, 96, 1))
    pieces = []
    for p in range(per // 2):
        pieces += [w[p : p + 1] for w in (k1re, k1im, k2re, k2im)]
    e_ref[me] = jnp.concatenate(pieces, axis=0)

    def e_send(i, carry):
        to = freq_peer(i)
        spread(e_ref, e_s, e_r, me, to, {"freq": to}).start()
        return carry

    lax.fori_loop(0, NC - 1, e_send, 0)

    own = lanes((2 * per, block)) // 64 == lanes((2 * per, block), 0) // 2

    def project(owner):
        e = e_ref[owner]
        left = jnp.where(own, jnp.concatenate([e] * (block // 128), axis=1), 0.0)
        high, low = split(left)
        first = pl.multiple_of(owner * block, block)
        right = ah_ref[pl.ds(first, block), :]
        both = dot(jnp.concatenate([high, low], axis=0), right)
        out = both[: 2 * per] + both[2 * per :] + dot(high, al_ref[pl.ds(first, block), :])
        return out * inv_root

    mr_ref[me] = project(me)

    for d in range(1, nz):
        other = (zc + d) % nz
        arrival(gz_ref, gz_s, gz_r, other, z_dev(other)).wait_recv()
    gf_ref[yc] = total_of(gz_ref, nz) * (1.0 / total_rows)
    for d in range(1, NY):
        other = (yc + d) % NY
        spread(gf_ref, ga_s, ga_r, yc, other, y_dev(other)).start()

    def modes_copy(to, slot):
        return pltpu.make_async_remote_copy(
            src_ref=ms_ref.at[to],
            dst_ref=mr_ref.at[slot],
            send_sem=m_s.at[to],
            recv_sem=m_r.at[slot],
            device_id={"freq": to},
            device_id_type=MESH,
        )

    def mode_step(i, carry):
        owner = freq_peer(i)
        arrival(e_ref, e_s, e_r, owner, {"freq": owner}).wait_recv()
        ms_ref[owner] = project(owner)
        modes_copy(owner, me).start()
        return carry

    lax.fori_loop(0, NC - 1, mode_step, 0)

    for d in range(1, NY):
        other = (yc + d) % NY
        arrival(gf_ref, ga_s, ga_r, other, y_dev(other)).wait_recv()
    for p in range(per // 2):
        step = NB // gsub
        g = jnp.concatenate([gf_ref[p * step + j] for j in range(step)], axis=0)
        for k in range(2):
            for c in range(2):
                row = ((2 * p + k) * 2 + c) * NB
                shift = (128 - (c * 64 + k * 32)) % 128
                turned = g if shift == 0 else pltpu.roll(g, shift, 1)
                gram_out[row : row + NB, :] = turned[:, :NB]

    def modes_wait(i, carry):
        sender = freq_peer(i)
        modes_copy(sender, sender).wait_recv()
        return carry

    lax.fori_loop(0, NC - 1, modes_wait, 0)
    for s in range(NC):
        modes_out[:, s * rows : (s + 1) * rows] = mr_ref[s]

    def sent_x(i, carry):
        to = freq_peer(i)
        gram_copy(to, me).wait_send()
        spread(e_ref, e_s, e_r, me, to, {"freq": to}).wait_send()
        modes_copy(to, me).wait_send()
        return carry

    lax.fori_loop(0, NC - 1, sent_x, 0)
    for d in range(1, NY):
        other = (yc + d) % NY
        spread(vy_ref, vy_s, vy_r, yc, other, y_dev(other)).wait_send()
        gram_y(other, yc).wait_send()
        spread(gf_ref, ga_s, ga_r, yc, other, y_dev(other)).wait_send()
    for d in range(1, nz):
        other = (zc + d) % nz
        spread(vz_ref, vz_s, vz_r, zc, other, z_dev(other)).wait_send()
        spread(gz_ref, gz_s, gz_r, zc, other, z_dev(other)).wait_send()


def shards(nz, table, snapshots, weight, start_vec):
    times, rows = snapshots.shape
    total_rows = weight.shape[0] * lax.axis_size("pts")
    per = NF // NC
    dma = pltpu.SemaphoreType.DMA
    vmem = pl.BlockSpec(memory_space=pltpu.VMEM)
    gram_rows = per // 2 * NB
    gram, modes = pl.pallas_call(
        functools.partial(kernel, nz, total_rows),
        out_shape=(
            jax.ShapeDtypeStruct((per * 2 * NB, NB), F32),
            jax.ShapeDtypeStruct((per * 2, NC * rows), F32),
        ),
        in_specs=[pl.BlockSpec(memory_space=pl.ANY), vmem, vmem, vmem],
        out_specs=(vmem, vmem),
        scratch_shapes=[
            pltpu.VMEM((times, rows), F32),
            pltpu.VMEM((times * 2, rows), BF),
            pltpu.VMEM((rows // 128, NF * 2 * NB, 128), F32),
            pltpu.VMEM((NF * 2 * NB, rows), BF),
            pltpu.VMEM((NF * 2 * NB, rows), BF),
            pltpu.VMEM((NC, gram_rows, 128), F32),
            pltpu.VMEM((NC, gram_rows, 128), F32),
            pltpu.VMEM((gram_rows, 128), F32),
            pltpu.VMEM((NY, gram_rows // NY, 128), F32),
            pltpu.VMEM((nz, gram_rows // NY, 128), F32),
            pltpu.VMEM((NY, gram_rows // NY, 128), F32),
            pltpu.VMEM((NY, per, 128), F32),
            pltpu.VMEM((nz, per, 128), F32),
            pltpu.VMEM((NC, per * 2, 128), F32),
            pltpu.VMEM((NC, per * 2, rows), F32),
            pltpu.VMEM((NC, per * 2, rows), F32),
            pltpu.VMEM((per // 2, NB, 128), F32),
            pltpu.VMEM((per // 2, NB, 128), F32),
            dma((8,)),
            dma((NC,)),
            dma((NC,)),
            dma((NY,)),
            dma((NY,)),
            dma((nz,)),
            dma((nz,)),
            dma((NY,)),
            dma((NY,)),
            dma((NY,)),
            dma((NY,)),
            dma((nz,)),
            dma((nz,)),
            dma((NC,)),
            dma((NC,)),
            dma((NC,)),
            dma((NC,)),
        ],
        compiler_params=pltpu.CompilerParams(collective_id=0, has_side_effects=True),
        name="spod",
    )(snapshots, weight.reshape(-1, 128), start_vec, table)
    return gram.reshape(per, 2, NB, NB), modes.reshape(per, 2, NC * rows)


def solution(mesh):
    placed = (P(None, ("pts", "freq")), P("pts"), P())
    nz = mesh.shape["pts"] // NY
    return jax.shard_map(
        functools.partial(shards, nz, dft_operand()),
        mesh=mesh,
        in_specs=placed,
        out_specs=(P("freq", None, None, None), P("freq", None, "pts")),
        check_vma=False,
    )
```

profile of v0, /device:TPU:1, one launch (start us, length us, event | category | flops | bytes accessed | tf_op | source)
XLA Modules:
  0.0 62.2 jit_solution(589152007850825907)
XLA Ops:
  0.6 1.5 %copy.6.start_ref = f32[64,2,32]{2,1,0:T(2,128)} copy(f32[64,2,32]{0,2,1:T(8,128)} %param.6) | data formatting | bytes 32768 | tf_op args[2]
  2.1 56.7 %spod.1 = (f32[512,32]{1,0:T(8,128)}, f32[16,3072]{1,0:T(8,128)}) custom-call(f32[2112,384]{1,0:T(8,128)} %snap_hbm.1, f32[24,128]{1,0:T(8,128)} %bitcast.3, f32[64,2,32]{2,1,0:T(2,128)} %copy.6.start_ref, bf16[256,256]{1,0:T(8,128)(2,1)} %constant.2.clone.table_ref), custom_call_target="tpu_custom_call" | custom-call | tf_op jit(solution)/shard_map/spod/pallas_call | solution.py:436
  58.8 1.7 %reshape.15 = f32[8,2,3072]{2,1,0:T(2,128)} reshape(f32[16,3072]{1,0:T(8,128)} %get-tuple-element.5) | data formatting | bytes 393216 | tf_op jit(solution)/shard_map/reshape | solution.py:484
  60.5 1.7 %copy.8 = f32[8,2,32,32]{3,2,1,0:T(8,128)} copy(f32[8,2,32,32]{3,2,1,0:T(8,128)} %bitcast.2) | data formatting | bytes 131072
where the time goes:
time: 62.4 us; the launch traced here: 62.2 us
  Pallas kernels  56.7 us (91%)
  local copies, waits for them, and re-layouts  4.86 us (8%)
  between operations  0.64 us (1%)
    pallas_call x1, Pallas kernels, shards(): pl.pallas_call(functools.partial(kernel, nz, total_rows), out_shape=(jax....  56.7 us
    unnamed x2, local copies, waits for them, and re-layouts  3.14 us
    reshape x1, local copies, waits for them, and re-layouts, shards(): return (gram.reshape(per, 2, NB, NB), modes.reshape(per, 2, NC * rows))  1.71 us

commit v1 on v0

--- a/solution.py
+++ b/solution.py
@@ -15,6 +15,7 @@
 HALF = NFFT // 2
 NC = 8
 NY = 8
+PITCH = NB + 1
 MESH = pl.DeviceIdType.MESH
 BF = jnp.bfloat16
 F32 = jnp.float32
@@ -68,6 +69,8 @@
     al_ref,
     gs_ref,
     gr_ref,
+    vs_ref,
+    vx_ref,
     gx_ref,
     gy_ref,
     gz_ref,
@@ -88,6 +91,8 @@
     gz_r,
     ga_s,
     ga_r,
+    vx_s,
+    vx_r,
     vy_s,
     vy_r,
     vz_s,
@@ -137,19 +142,23 @@
     )
     root = jnp.sqrt(weight)
     inv_root = 1.0 / root
-    eye = lanes((NB, NB), 0) == lanes((NB, NB), 1)
-
-    def column(k, c):
-        row = start_ref[me * (NF // NC) + k, pl.ds(c, 1), :]
-        col = jnp.sum(jnp.where(eye, row, 0.0), axis=1, keepdims=True)
-        return jnp.broadcast_to(col, (NB, 128))
-
     seg = lanes((NB, 128)) // 32
-    for p in range(NF // NC // 2):
-        r1, i1 = column(2 * p, 0), column(2 * p, 1)
-        r2, i2 = column(2 * p + 1, 0), column(2 * p + 1, 1)
-        sa_ref[p] = jnp.where(seg == 0, r1, jnp.where(seg == 1, r2, jnp.where(seg == 2, i1, i2)))
-        sb_ref[p] = jnp.where(seg == 0, i1, jnp.where(seg == 1, i2, jnp.where(seg == 2, -r1, -r2)))
+    coeffs = jnp.concatenate([start_ref[0], start_ref[1]], axis=1)
+
+    def tables(i, carry):
+        turned = pltpu.roll(coeffs, 128 - 4 * i, 1)
+        for odd in range(2):
+            r1, r2, i1, i2 = (
+                jnp.broadcast_to(turned[:, n : n + 1], (NB, 128))
+                for n in (2 * odd, 2 * odd + 1, 64 + 2 * odd, 65 + 2 * odd)
+            )
+            at = seg if odd == 0 else (seg + 2) % 4
+            pair = 2 * i + odd
+            sa_ref[pair] = jnp.where(at == 0, r1, jnp.where(at == 1, r2, jnp.where(at == 2, i1, i2)))
+            sb_ref[pair] = jnp.where(at == 0, i1, jnp.where(at == 1, i2, jnp.where(at == 2, -r1, -r2)))
+        return carry
+
+    lax.fori_loop(0, NF // 4, tables, 0)
 
     total = jnp.zeros((24, rows), F32)
     for i in range(chunks):
@@ -159,7 +168,7 @@
     mean = jnp.sum(total, axis=0, keepdims=True) * (1.0 / x_ref.shape[0])
 
     def centre(j):
-        high, low = split(x_ref[pl.ds(pl.multiple_of(j * HALF, HALF), HALF), :] - mean)
+        high, low = split((x_ref[pl.ds(pl.multiple_of(j * HALF, HALF), HALF), :] - mean) * root)
         xc_ref[pl.ds(pl.multiple_of(j * NFFT, NFFT), HALF), :] = high
         xc_ref[pl.ds(pl.multiple_of(j * NFFT + HALF, HALF), HALF), :] = low
 
@@ -168,9 +177,9 @@
 
     def transform(b, carry):
         both = dot(table_ref[...], xc_ref[pl.ds(pl.multiple_of(b * NFFT, NFFT), 2 * NFFT), :])
-        value = (both[: 2 * NF] + both[2 * NF :]) * root
+        value = both[: 2 * NF] + both[2 * NF :]
         for j in range(groups):
-            q_ref[j, pl.ds(b, 2 * NF, stride=NB), :] = value[:, j * 128 : (j + 1) * 128]
+            q_ref[j, pl.ds(b, 2 * NF, stride=PITCH), :] = value[:, j * 128 : (j + 1) * 128]
         centre(jnp.minimum(b + 2, halves - 1))
         return carry
 
@@ -191,57 +200,82 @@
             device_id_type=MESH,
         )
 
+    def vx_copy(to, slot):
+        return pltpu.make_async_remote_copy(
+            src_ref=vs_ref.at[to],
+            dst_ref=vx_ref.at[slot],
+            send_sem=vx_s.at[to],
+            recv_sem=vx_r.at[slot],
+            device_id={"freq": to},
+            device_id_type=MESH,
+        )
+
+    upper = lanes((NB, 128), 0) <= lanes((NB, 128)) % 32
+    lane4 = lanes((per // 2, 128))
+    lane = lanes((NB, 128))
+
     def gram_of(owner):
+        parts_a, parts_b, packed = [], [], None
         for p in range(per // 2):
             first = pl.multiple_of(owner * block + p * 128, 128)
-            value = [q_ref[j, pl.ds(first, 128), :] for j in range(groups)]
-            high, low = split(jnp.concatenate(value, axis=1))
-            ah_ref[pl.ds(first, 128), :] = high
-            al_ref[pl.ds(first, 128), :] = low
-
-            def reim(v):
-                return (
-                    jnp.concatenate([v[0:32], v[64:96]], axis=0),
-                    jnp.concatenate([v[32:64], v[96:128]], axis=0),
-                )
-
-            rh, ih = reim(high)
-            rl, il = reim(low)
+            for n in range(4):
+                source = (owner * (2 * per) + p * 4 + n) * PITCH
+                value = [q_ref[j, pl.ds(source, NB), :] for j in range(groups)]
+                high, low = split(jnp.concatenate(value, axis=1))
+                ah_ref[pl.ds(first + n * NB, NB), :] = high
+                al_ref[pl.ds(first + n * NB, NB), :] = low
+
+            def reim(ref):
+                v = [ref[pl.ds(first + n * NB, NB), :] for n in range(4)]
+                return jnp.concatenate([v[0], v[2]], axis=0), jnp.concatenate([v[1], v[3]], axis=0)
+
+            rh, ih = reim(ah_ref)
+            rl, il = reim(al_ref)
             h1 = jnp.concatenate([rh, ih], axis=1)
             l1 = jnp.concatenate([rl, il], axis=1)
             h2 = jnp.concatenate([ih, -rh], axis=1)
             l2 = jnp.concatenate([il, -rl], axis=1)
-            out = dot_t(
-                jnp.concatenate([h1, l1], axis=0), jnp.concatenate([h1, h2, l1, l2], axis=0)
-            )
+            right = [h1, h2, l1, l2] if p % 2 == 0 else [h2, h1, l2, l1]
+            out = dot_t(jnp.concatenate([h1, l1], axis=0), jnp.concatenate(right, axis=0))
             z = out[0:64, 0:128] + (out[0:64, 128:256] + out[64:128, 0:128])
-            gs_ref[owner, pl.ds(p * NB, NB), :] = jnp.where(seg % 2 == 0, z[0:32], z[32:64])
+            g = jnp.where(seg % 2 == 0, z[0:32], z[32:64])
+            pair = owner * (per // 2) + p
+            parts_a.append(jnp.sum(g * sa_ref[pair], axis=0, keepdims=True))
+            parts_b.append(jnp.sum(g * sb_ref[pair], axis=0, keepdims=True))
+            half = jnp.where(upper, g, pltpu.roll(g, 64, 1))
+            if p % 2 == 0:
+                packed = half
+            else:
+                both = jnp.where(lane < 64, packed, half)
+                gs_ref[owner, pl.ds(p // 2 * NB, NB), :] = both
+        va = jnp.concatenate(parts_a, axis=0)
+        vb = jnp.concatenate(parts_b, axis=0)
+        vs_ref[owner] = jnp.where(
+            lane4 < 64, va + pltpu.roll(va, 64, 1), vb + pltpu.roll(vb, 64, 1)
+        )
 
     def gram_step(i, carry):
         owner = freq_peer(i)
         gram_of(owner)
+        vx_copy(owner, me).start()
         gram_copy(owner, me).start()
         return carry
 
     lax.fori_loop(0, NC - 1, gram_step, 0)
     gram_of(me)
-
-    gx_ref[...] = gs_ref[me]
-
-    def gram_sum(i, carry):
-        sender = ((xc + 1 + i // 2) % (NC // 2)) * 2 + (core + 1 - i % 2) % 2
-        gram_copy(sender, sender).wait_recv()
-        gx_ref[...] += gr_ref[sender]
-        return carry
-
-    lax.fori_loop(0, NC - 1, gram_sum, 0)
-
-    parts_a, parts_b = [], []
-    for p in range(per // 2):
-        g = gx_ref[p * NB : (p + 1) * NB, :]
-        parts_a.append(jnp.sum(g * sa_ref[p], axis=0, keepdims=True))
-        parts_b.append(jnp.sum(g * sb_ref[p], axis=0, keepdims=True))
-    vy_ref[yc] = jnp.concatenate(parts_a + parts_b, axis=0)
+    vx_ref[me] = vs_ref[me]
+    gr_ref[me] = gs_ref[me]
+
+    def total_of(buf, n):
+        out = buf[0]
+        for i in range(1, n):
+            out = out + buf[i]
+        return out
+
+    for i in range(NC - 1):
+        sender = freq_peer(i)
+        vx_copy(sender, sender).wait_recv()
+    vy_ref[yc] = total_of(vx_ref, NC)
 
     gsub = gx_ref.shape[0] // NY
 
@@ -271,15 +305,14 @@
             device_id_type=MESH,
         )
 
-    def total_of(buf, n):
-        out = buf[0]
-        for i in range(1, n):
-            out = out + buf[i]
-        return out
-
     for d in range(1, NY):
         other = (yc + d) % NY
         spread(vy_ref, vy_s, vy_r, yc, other, y_dev(other)).start()
+
+    for i in range(NC - 1):
+        sender = freq_peer(i)
+        gram_copy(sender, sender).wait_recv()
+    gx_ref[...] = total_of(gr_ref, NC)
 
     def gram_y(other, slot):
         return pltpu.make_async_remote_copy(
@@ -316,14 +349,14 @@
         arrival(vz_ref, vz_s, vz_r, other, z_dev(other)).wait_recv()
     v = total_of(vz_ref, nz) * (1.0 / total_rows)
 
-    lane = lanes((per // 2, 128))
-    odd = (lane // 32) % 2 == 1
-    va, vb = v[0 : per // 2], v[per // 2 :]
-    vr = va + pltpu.roll(va, 64, 1)
-    vi = vb + pltpu.roll(vb, 64, 1)
-    square = vr * vr + vi * vi
-    norm1 = jnp.sum(jnp.where(lane < 32, square, 0.0), axis=1, keepdims=True) * (1.0 / NB)
-    norm2 = jnp.sum(jnp.where((lane >= 32) & (lane < 64), square, 0.0), axis=1, keepdims=True)
+    odd = (lane4 // 32) % 2 == 1
+    turned = pltpu.roll(v, 64, 1)
+    vr = jnp.where(lane4 < 64, v, turned)
+    vi = jnp.where(lane4 < 64, turned, v)
+    square = v * v
+    square = square + pltpu.roll(square, 64, 1)
+    norm1 = jnp.sum(jnp.where(lane4 < 32, square, 0.0), axis=1, keepdims=True) * (1.0 / NB)
+    norm2 = jnp.sum(jnp.where((lane4 >= 32) & (lane4 < 64), square, 0.0), axis=1, keepdims=True)
     norm2 = norm2 * (1.0 / NB)
     scale = jnp.where(odd, 1.0 / jnp.sqrt(norm2 + 1e-06), 1.0 / jnp.sqrt(norm1 + 1e-06))
     yr = vr * scale
@@ -388,15 +421,21 @@
     for d in range(1, NY):
         other = (yc + d) % NY
         arrival(gf_ref, ga_s, ga_r, other, y_dev(other)).wait_recv()
-    for p in range(per // 2):
-        step = NB // gsub
-        g = jnp.concatenate([gf_ref[p * step + j] for j in range(step)], axis=0)
-        for k in range(2):
-            for c in range(2):
-                row = ((2 * p + k) * 2 + c) * NB
-                shift = (128 - (c * 64 + k * 32)) % 128
-                turned = g if shift == 0 else pltpu.roll(g, shift, 1)
-                gram_out[row : row + NB, :] = turned[:, :NB]
+    packed = jnp.concatenate([gf_ref[i] for i in range(NY)], axis=0)
+    flipped = jnp.concatenate([packed, packed], axis=0).T
+    for q in range(per // 4):
+        for k in range(4):
+            here = packed[q * NB : (q + 1) * NB]
+            there = flipped[k * NB : (k + 1) * NB]
+            here = here if k == 0 else pltpu.roll(here, 128 - 32 * k, 1)
+            there = there if q == 0 else pltpu.roll(there, 128 - 32 * q, 1)
+            row = (4 * q + k) * 2 * NB
+            above = lanes((NB, NB), 0) <= lanes((NB, NB))
+            same = lanes((NB, NB), 0) == lanes((NB, NB))
+            here, there = here[:, :NB], there[:, :NB]
+            gram_out[row : row + NB, :] = jnp.where(above, here, there)
+            imag = jnp.where(above, -there, here)
+            gram_out[row + NB : row + 2 * NB, :] = jnp.where(same, 0.0, imag)
 
     def modes_wait(i, carry):
         sender = freq_peer(i)
@@ -410,6 +449,7 @@
     def sent_x(i, carry):
         to = freq_peer(i)
         gram_copy(to, me).wait_send()
+        vx_copy(to, me).wait_send()
         spread(e_ref, e_s, e_r, me, to, {"freq": to}).wait_send()
         modes_copy(to, me).wait_send()
         return carry
@@ -432,7 +472,7 @@
     per = NF // NC
     dma = pltpu.SemaphoreType.DMA
     vmem = pl.BlockSpec(memory_space=pltpu.VMEM)
-    gram_rows = per // 2 * NB
+    gram_rows = per // 4 * NB
     gram, modes = pl.pallas_call(
         functools.partial(kernel, nz, total_rows),
         out_shape=(
@@ -444,22 +484,24 @@
         scratch_shapes=[
             pltpu.VMEM((times, rows), F32),
             pltpu.VMEM((times * 2, rows), BF),
-            pltpu.VMEM((rows // 128, NF * 2 * NB, 128), F32),
+            pltpu.VMEM((rows // 128, NF * 2 * PITCH, 128), F32),
             pltpu.VMEM((NF * 2 * NB, rows), BF),
             pltpu.VMEM((NF * 2 * NB, rows), BF),
             pltpu.VMEM((NC, gram_rows, 128), F32),
             pltpu.VMEM((NC, gram_rows, 128), F32),
+            pltpu.VMEM((NC, per // 2, 128), F32),
+            pltpu.VMEM((NC, per // 2, 128), F32),
             pltpu.VMEM((gram_rows, 128), F32),
             pltpu.VMEM((NY, gram_rows // NY, 128), F32),
             pltpu.VMEM((nz, gram_rows // NY, 128), F32),
             pltpu.VMEM((NY, gram_rows // NY, 128), F32),
-            pltpu.VMEM((NY, per, 128), F32),
-            pltpu.VMEM((nz, per, 128), F32),
+            pltpu.VMEM((NY, per // 2, 128), F32),
+            pltpu.VMEM((nz, per // 2, 128), F32),
             pltpu.VMEM((NC, per * 2, 128), F32),
             pltpu.VMEM((NC, per * 2, rows), F32),
             pltpu.VMEM((NC, per * 2, rows), F32),
-            pltpu.VMEM((per // 2, NB, 128), F32),
-            pltpu.VMEM((per // 2, NB, 128), F32),
+            pltpu.VMEM((NF // 2, NB, 128), F32),
+            pltpu.VMEM((NF // 2, NB, 128), F32),
             dma((8,)),
             dma((NC,)),
             dma((NC,)),
@@ -469,6 +511,8 @@
             dma((nz,)),
             dma((NY,)),
             dma((NY,)),
+            dma((NC,)),
+            dma((NC,)),
             dma((NY,)),
             dma((NY,)),
             dma((nz,)),
@@ -480,7 +524,7 @@
         ],
         compiler_params=pltpu.CompilerParams(collective_id=0, has_side_effects=True),
         name="spod",
-    )(snapshots, weight.reshape(-1, 128), start_vec, table)
+    )(snapshots, weight.reshape(-1, 128), start_vec.transpose(1, 2, 0), table)
     return gram.reshape(per, 2, NB, NB), modes.reshape(per, 2, NC * rows)
 
 

time: 62.4 us -> 55.1 us (0.88)
  Pallas kernels: 56.7 us -> 50.9 us
  local copies, waits for them, and re-layouts: 4.86 us -> 3.38 us
    pallas_call x1, Pallas kernels: 56.7 us -> 50.9 us  [shards(): pl.pallas_call(functools.partial(kernel, nz, total_rows), out_shape=(jax....]
    unnamed x2 -> x1, local copies, waits for them, and re-layouts: 3.14 us -> 1.67 us
where the time goes in v1:
time: 55.1 us; the launch traced here: 54.9 us
  Pallas kernels  50.9 us (92%)
  local copies, waits for them, and re-layouts  3.38 us (6%)
  between operations  0.64 us (1%)
    pallas_call x1, Pallas kernels, shards(): pl.pallas_call(functools.partial(kernel, nz, total_rows), out_shape=(jax....  50.9 us
    reshape x1, local copies, waits for them, and re-layouts, shards(): return (gram.reshape(per, 2, NB, NB), modes.reshape(per, 2, NC * rows))  1.71 us
    unnamed x1, local copies, waits for them, and re-layouts  1.67 us

profile of v1, /device:TPU:1, one launch (start us, length us, event | category | flops | bytes accessed | tf_op | source)
XLA Modules:
  0.0 54.9 jit_solution(10347249378310164589)
XLA Ops:
  0.6 50.9 %spod.1 = (f32[512,32]{1,0:T(8,128)}, f32[16,3072]{1,0:T(8,128)}) custom-call(f32[2112,384]{1,0:T(8,128)} %snap_hbm.1, f32[24,128]{1,0:T(8,128)} %bitcast.5, f32[2,32,64]{2,1,0:T(8,128)} %bitcast.4, bf16[256,256]{1,0:T(8,128)(2,1)} %constant.2.clone.table_ref), custom_call_target="tpu_custom_call" | custom-call | tf_op jit(solution)/shard_map/spod/pallas_call | solution.py:476
  51.5 1.7 %reshape.15 = f32[8,2,3072]{2,1,0:T(2,128)} reshape(f32[16,3072]{1,0:T(8,128)} %get-tuple-element.5) | data formatting | bytes 393216 | tf_op jit(solution)/shard_map/reshape | solution.py:528
  53.3 1.7 %copy.7 = f32[8,2,32,32]{3,2,1,0:T(8,128)} copy(f32[8,2,32,32]{3,2,1,0:T(8,128)} %bitcast.3) | data formatting | bytes 131072

commit v2 on v1

--- a/solution.py
+++ b/solution.py
@@ -122,7 +122,8 @@
         load(i).start()
 
     def freq_peer(i):
-        return ((xc + 3 - i // 2) % (NC // 2)) * 2 + (core + 1 - i % 2) % 2
+        step = (2, 1, 3, 0)[i // 2]
+        return ((xc + step) % (NC // 2)) * 2 + (core + 1 - i % 2) % 2
 
     barrier = pltpu.get_barrier_semaphore()
     for i in range(NC - 1):
@@ -145,20 +146,16 @@
     seg = lanes((NB, 128)) // 32
     coeffs = jnp.concatenate([start_ref[0], start_ref[1]], axis=1)
 
-    def tables(i, carry):
-        turned = pltpu.roll(coeffs, 128 - 4 * i, 1)
+    for i in range(NF // 4):
         for odd in range(2):
             r1, r2, i1, i2 = (
-                jnp.broadcast_to(turned[:, n : n + 1], (NB, 128))
-                for n in (2 * odd, 2 * odd + 1, 64 + 2 * odd, 65 + 2 * odd)
+                jnp.broadcast_to(coeffs[:, n : n + 1], (NB, 128))
+                for n in (4 * i + 2 * odd, 4 * i + 2 * odd + 1, NF + 4 * i + 2 * odd, NF + 4 * i + 2 * odd + 1)
             )
             at = seg if odd == 0 else (seg + 2) % 4
             pair = 2 * i + odd
             sa_ref[pair] = jnp.where(at == 0, r1, jnp.where(at == 1, r2, jnp.where(at == 2, i1, i2)))
             sb_ref[pair] = jnp.where(at == 0, i1, jnp.where(at == 1, i2, jnp.where(at == 2, -r1, -r2)))
-        return carry
-
-    lax.fori_loop(0, NF // 4, tables, 0)
 
     total = jnp.zeros((24, rows), F32)
     for i in range(chunks):
@@ -168,22 +165,24 @@
     mean = jnp.sum(total, axis=0, keepdims=True) * (1.0 / x_ref.shape[0])
 
     def centre(j):
-        high, low = split((x_ref[pl.ds(pl.multiple_of(j * HALF, HALF), HALF), :] - mean) * root)
-        xc_ref[pl.ds(pl.multiple_of(j * NFFT, NFFT), HALF), :] = high
-        xc_ref[pl.ds(pl.multiple_of(j * NFFT + HALF, HALF), HALF), :] = low
-
-    centre(0)
-    centre(1)
-
-    def transform(b, carry):
-        both = dot(table_ref[...], xc_ref[pl.ds(pl.multiple_of(b * NFFT, NFFT), 2 * NFFT), :])
+        high, low = split((x_ref[j * HALF : (j + 1) * HALF, :] - mean) * root)
+        xc_ref[j * NFFT : j * NFFT + HALF, :] = high
+        xc_ref[j * NFFT + HALF : (j + 1) * NFFT, :] = low
+
+    done = 0
+    for b in range(0, NB, 2):
+        while done < min(b + 3 + 2, halves):
+            centre(done)
+            done += 1
+        right = jnp.concatenate(
+            [xc_ref[n * NFFT : (n + 2) * NFFT, :] for n in (b, b + 1)], axis=1
+        )
+        both = dot(table_ref[...], right)
         value = both[: 2 * NF] + both[2 * NF :]
-        for j in range(groups):
-            q_ref[j, pl.ds(b, 2 * NF, stride=PITCH), :] = value[:, j * 128 : (j + 1) * 128]
-        centre(jnp.minimum(b + 2, halves - 1))
-        return carry
-
-    lax.fori_loop(0, NB, transform, 0)
+        for m in range(2):
+            for j in range(groups):
+                at = m * rows + j * 128
+                q_ref[j, pl.ds(b + m, 2 * NF, stride=PITCH), :] = value[:, at : at + 128]
 
     pl.semaphore_wait(barrier, NC - 1 + NY - 1 + nz - 1)
 
@@ -214,29 +213,33 @@
     lane4 = lanes((per // 2, 128))
     lane = lanes((NB, 128))
 
+    def split_of(owner, p):
+        first = pl.multiple_of(owner * block + p * 128, 128)
+        hs, ls = [], []
+        for n in range(4):
+            source = (owner * (2 * per) + p * 4 + n) * PITCH
+            value = [q_ref[j, pl.ds(source, NB), :] for j in range(groups)]
+            high, low = split(jnp.concatenate(value, axis=1))
+            ah_ref[pl.ds(first + n * NB, NB), :] = high
+            al_ref[pl.ds(first + n * NB, NB), :] = low
+            hs.append(high); ls.append(low)
+        return hs, ls
+
+    def operands(hs, ls, p):
+        rh, ih = jnp.concatenate([hs[0], hs[2]], axis=0), jnp.concatenate([hs[1], hs[3]], axis=0)
+        rl, il = jnp.concatenate([ls[0], ls[2]], axis=0), jnp.concatenate([ls[1], ls[3]], axis=0)
+        h1 = jnp.concatenate([rh, ih], axis=1)
+        l1 = jnp.concatenate([rl, il], axis=1)
+        h2 = jnp.concatenate([ih, -rh], axis=1)
+        l2 = jnp.concatenate([il, -rl], axis=1)
+        right = [h1, h2, l1, l2] if p % 2 == 0 else [h2, h1, l2, l1]
+        return jnp.concatenate([h1, l1], axis=0), jnp.concatenate(right, axis=0)
+
     def gram_of(owner):
         parts_a, parts_b, packed = [], [], None
         for p in range(per // 2):
-            first = pl.multiple_of(owner * block + p * 128, 128)
-            for n in range(4):
-                source = (owner * (2 * per) + p * 4 + n) * PITCH
-                value = [q_ref[j, pl.ds(source, NB), :] for j in range(groups)]
-                high, low = split(jnp.concatenate(value, axis=1))
-                ah_ref[pl.ds(first + n * NB, NB), :] = high
-                al_ref[pl.ds(first + n * NB, NB), :] = low
-
-            def reim(ref):
-                v = [ref[pl.ds(first + n * NB, NB), :] for n in range(4)]
-                return jnp.concatenate([v[0], v[2]], axis=0), jnp.concatenate([v[1], v[3]], axis=0)
-
-            rh, ih = reim(ah_ref)
-            rl, il = reim(al_ref)
-            h1 = jnp.concatenate([rh, ih], axis=1)
-            l1 = jnp.concatenate([rl, il], axis=1)
-            h2 = jnp.concatenate([ih, -rh], axis=1)
-            l2 = jnp.concatenate([il, -rl], axis=1)
-            right = [h1, h2, l1, l2] if p % 2 == 0 else [h2, h1, l2, l1]
-            out = dot_t(jnp.concatenate([h1, l1], axis=0), jnp.concatenate(right, axis=0))
+            left, right = operands(*split_of(owner, p), p)
+            out = dot_t(left, right)
             z = out[0:64, 0:128] + (out[0:64, 128:256] + out[64:128, 0:128])
             g = jnp.where(seg % 2 == 0, z[0:32], z[32:64])
             pair = owner * (per // 2) + p
@@ -254,14 +257,14 @@
             lane4 < 64, va + pltpu.roll(va, 64, 1), vb + pltpu.roll(vb, 64, 1)
         )
 
-    def gram_step(i, carry):
+    def gram_step(i):
         owner = freq_peer(i)
         gram_of(owner)
         vx_copy(owner, me).start()
         gram_copy(owner, me).start()
-        return carry
-
-    lax.fori_loop(0, NC - 1, gram_step, 0)
+
+    for i in range(NC - 1):
+        gram_step(i)
     gram_of(me)
     vx_ref[me] = vs_ref[me]
     gr_ref[me] = gs_ref[me]
@@ -370,12 +373,9 @@
         pieces += [w[p : p + 1] for w in (k1re, k1im, k2re, k2im)]
     e_ref[me] = jnp.concatenate(pieces, axis=0)
 
-    def e_send(i, carry):
+    for i in range(NC - 1):
         to = freq_peer(i)
         spread(e_ref, e_s, e_r, me, to, {"freq": to}).start()
-        return carry
-
-    lax.fori_loop(0, NC - 1, e_send, 0)
 
     own = lanes((2 * per, block)) // 64 == lanes((2 * per, block), 0) // 2
 
@@ -409,14 +409,15 @@
             device_id_type=MESH,
         )
 
-    def mode_step(i, carry):
-        owner = freq_peer(i)
-        arrival(e_ref, e_s, e_r, owner, {"freq": owner}).wait_recv()
-        ms_ref[owner] = project(owner)
-        modes_copy(owner, me).start()
-        return carry
-
-    lax.fori_loop(0, NC - 1, mode_step, 0)
+    for step in ((6,), (2, 3), (4, 5), (0, 1)):
+        owners = [freq_peer(i) for i in step]
+        for owner in owners:
+            arrival(e_ref, e_s, e_r, owner, {"freq": owner}).wait_recv()
+        values = [project(owner) for owner in owners]
+        for owner, value in zip(owners, values):
+            ms_ref[owner] = value
+        for owner in owners:
+            modes_copy(owner, me).start()
 
     for d in range(1, NY):
         other = (yc + d) % NY
@@ -437,24 +438,11 @@
             imag = jnp.where(above, -there, here)
             gram_out[row + NB : row + 2 * NB, :] = jnp.where(same, 0.0, imag)
 
-    def modes_wait(i, carry):
-        sender = freq_peer(i)
-        modes_copy(sender, sender).wait_recv()
-        return carry
-
-    lax.fori_loop(0, NC - 1, modes_wait, 0)
-    for s in range(NC):
-        modes_out[:, s * rows : (s + 1) * rows] = mr_ref[s]
-
-    def sent_x(i, carry):
+    for i in range(NC - 1):
         to = freq_peer(i)
         gram_copy(to, me).wait_send()
         vx_copy(to, me).wait_send()
         spread(e_ref, e_s, e_r, me, to, {"freq": to}).wait_send()
-        modes_copy(to, me).wait_send()
-        return carry
-
-    lax.fori_loop(0, NC - 1, sent_x, 0)
     for d in range(1, NY):
         other = (yc + d) % NY
         spread(vy_ref, vy_s, vy_r, yc, other, y_dev(other)).wait_send()
@@ -464,6 +452,14 @@
         other = (zc + d) % nz
         spread(vz_ref, vz_s, vz_r, zc, other, z_dev(other)).wait_send()
         spread(gz_ref, gz_s, gz_r, zc, other, z_dev(other)).wait_send()
+
+    for i in (6, 2, 3, 4, 5, 0, 1):
+        sender = freq_peer(i)
+        modes_copy(sender, sender).wait_recv()
+    for s in range(NC):
+        modes_out[:, s * rows : (s + 1) * rows] = mr_ref[s]
+    for i in range(NC - 1):
+        modes_copy(freq_peer(i), me).wait_send()
 
 
 def shards(nz, table, snapshots, weight, start_vec):

time: 55.1 us -> 46.9 us (0.85)
  Pallas kernels: 50.9 us -> 42.7 us
    pallas_call x1, Pallas kernels: 50.9 us -> 42.7 us  [shards(): pl.pallas_call(functools.partial(kernel, nz, total_rows), out_shape=(jax....]
where the time goes in v2:
time: 46.9 us; the launch traced here: 46.7 us
  Pallas kernels  42.7 us (91%)
  local copies, waits for them, and re-layouts  3.38 us (7%)
  between operations  0.64 us (1%)
    pallas_call x1, Pallas kernels, shards(): pl.pallas_call(functools.partial(kernel, nz, total_rows), out_shape=(jax....  42.7 us
    reshape x1, local copies, waits for them, and re-layouts, shards(): return (gram.reshape(per, 2, NB, NB), modes.reshape(per, 2, NC * rows))  1.71 us
    unnamed x1, local copies, waits for them, and re-layouts  1.67 us

profile of v2, /device:TPU:1, one launch (start us, length us, event | category | flops | bytes accessed | tf_op | source)
XLA Modules:
  0.0 46.7 jit_solution(6322005688327937697)
XLA Ops:
  0.6 42.7 %spod.1 = (f32[512,32]{1,0:T(8,128)}, f32[16,3072]{1,0:T(8,128)}) custom-call(f32[2112,384]{1,0:T(8,128)} %snap_hbm.1, f32[24,128]{1,0:T(8,128)} %bitcast.5, f32[2,32,64]{2,1,0:T(8,128)} %bitcast.4, bf16[256,256]{1,0:T(8,128)(2,1)} %constant.2.clone.table_ref), custom_call_target="tpu_custom_call" | custom-call | tf_op jit(solution)/shard_map/spod/pallas_call | solution.py:472
  43.3 1.7 %reshape.15 = f32[8,2,3072]{2,1,0:T(2,128)} reshape(f32[16,3072]{1,0:T(8,128)} %get-tuple-element.5) | data formatting | bytes 393216 | tf_op jit(solution)/shard_map/reshape | solution.py:524
  45.0 1.7 %copy.7 = f32[8,2,32,32]{3,2,1,0:T(8,128)} copy(f32[8,2,32,32]{3,2,1,0:T(8,128)} %bitcast.3) | data formatting | bytes 131072

commit v3 on v2

--- a/solution.py
+++ b/solution.py
@@ -57,11 +57,14 @@
     nz,
     total_rows,
     snap_hbm,
+    weight_hbm,
+    start_hbm,
+    table_hbm,
+    gram_out,
+    modes_out,
     weight_ref,
     start_ref,
     table_ref,
-    gram_out,
-    modes_out,
     x_ref,
     xc_ref,
     q_ref,
@@ -82,6 +85,7 @@
     mr_ref,
     sa_ref,
     sb_ref,
+    small_sem,
     load_sem,
     gx_s,
     gx_r,
@@ -118,8 +122,17 @@
         part = pl.ds(i * span, span)
         return pltpu.make_async_copy(snap_hbm.at[part, :], x_ref.at[part, :], load_sem.at[i])
 
+    small = [
+        pltpu.make_async_copy(source, target, small_sem.at[i])
+        for i, (source, target) in enumerate(
+            ((start_hbm, start_ref), (weight_hbm, weight_ref), (table_hbm, table_ref))
+        )
+    ]
+    for copy in small[:2]:
+        copy.start()
     for i in range(chunks):
         load(i).start()
+    small[2].start()
 
     def freq_peer(i):
         step = (2, 1, 3, 0)[i // 2]
@@ -136,6 +149,9 @@
         pl.semaphore_signal(
             barrier, inc=1, device_id={"pts": (zc + d) % nz * NY + yc}, device_id_type=MESH
         )
+
+    small[0].wait()
+    small[1].wait()
 
     groups = rows // 128
     weight = jnp.concatenate(
@@ -163,6 +179,8 @@
         for j in range(span // 24):
             total = total + x_ref[i * span + j * 24 : i * span + (j + 1) * 24, :]
     mean = jnp.sum(total, axis=0, keepdims=True) * (1.0 / x_ref.shape[0])
+
+    small[2].wait()
 
     def centre(j):
         high, low = split((x_ref[j * HALF : (j + 1) * HALF, :] - mean) * root)
@@ -422,21 +440,8 @@
     for d in range(1, NY):
         other = (yc + d) % NY
         arrival(gf_ref, ga_s, ga_r, other, y_dev(other)).wait_recv()
-    packed = jnp.concatenate([gf_ref[i] for i in range(NY)], axis=0)
-    flipped = jnp.concatenate([packed, packed], axis=0).T
-    for q in range(per // 4):
-        for k in range(4):
-            here = packed[q * NB : (q + 1) * NB]
-            there = flipped[k * NB : (k + 1) * NB]
-            here = here if k == 0 else pltpu.roll(here, 128 - 32 * k, 1)
-            there = there if q == 0 else pltpu.roll(there, 128 - 32 * q, 1)
-            row = (4 * q + k) * 2 * NB
-            above = lanes((NB, NB), 0) <= lanes((NB, NB))
-            same = lanes((NB, NB), 0) == lanes((NB, NB))
-            here, there = here[:, :NB], there[:, :NB]
-            gram_out[row : row + NB, :] = jnp.where(above, here, there)
-            imag = jnp.where(above, -there, here)
-            gram_out[row + NB : row + 2 * NB, :] = jnp.where(same, 0.0, imag)
+    for i in range(NY):
+        gram_out[i * gsub : (i + 1) * gsub, :] = gf_ref[i]
 
     for i in range(NC - 1):
         to = freq_peer(i)
@@ -457,9 +462,31 @@
         sender = freq_peer(i)
         modes_copy(sender, sender).wait_recv()
     for s in range(NC):
-        modes_out[:, s * rows : (s + 1) * rows] = mr_ref[s]
+        modes_out[s] = mr_ref[s]
     for i in range(NC - 1):
         modes_copy(freq_peer(i), me).wait_send()
+
+
+def finish(gram_ref, modes_ref, gram_out, modes_out):
+    rows = modes_ref.shape[2]
+    per = modes_ref.shape[1] // 2
+    for s in range(NC):
+        value = modes_ref[s]
+        for k in range(per):
+            modes_out[k, :, s * rows : (s + 1) * rows] = value[2 * k : 2 * k + 2]
+    packed = gram_ref[...]
+    flipped = jnp.concatenate([packed, packed], axis=0).T
+    above = lanes((NB, NB), 0) <= lanes((NB, NB))
+    same = lanes((NB, NB), 0) == lanes((NB, NB))
+    for q in range(per // 4):
+        for k in range(4):
+            here = packed[q * NB : (q + 1) * NB]
+            there = flipped[k * NB : (k + 1) * NB]
+            here = here if k == 0 else pltpu.roll(here, 128 - 32 * k, 1)
+            there = there if q == 0 else pltpu.roll(there, 128 - 32 * q, 1)
+            here, there = here[:, :NB], there[:, :NB]
+            gram_out[4 * q + k, 0] = jnp.where(above, here, there)
+            gram_out[4 * q + k, 1] = jnp.where(same, 0.0, jnp.where(above, -there, here))
 
 
 def shards(nz, table, snapshots, weight, start_vec):
@@ -472,12 +499,15 @@
     gram, modes = pl.pallas_call(
         functools.partial(kernel, nz, total_rows),
         out_shape=(
-            jax.ShapeDtypeStruct((per * 2 * NB, NB), F32),
-            jax.ShapeDtypeStruct((per * 2, NC * rows), F32),
+            jax.ShapeDtypeStruct((gram_rows, 128), F32),
+            jax.ShapeDtypeStruct((NC, per * 2, rows), F32),
         ),
-        in_specs=[pl.BlockSpec(memory_space=pl.ANY), vmem, vmem, vmem],
+        in_specs=[pl.BlockSpec(memory_space=pltpu.HBM)] * 4,
         out_specs=(vmem, vmem),
         scratch_shapes=[
+            pltpu.VMEM((weight.shape[0] // 128, 128), F32),
+            pltpu.VMEM((2, NB, NF), F32),
+            pltpu.VMEM(table.shape, BF),
             pltpu.VMEM((times, rows), F32),
             pltpu.VMEM((times * 2, rows), BF),
             pltpu.VMEM((rows // 128, NF * 2 * PITCH, 128), F32),
@@ -498,6 +528,7 @@
             pltpu.VMEM((NC, per * 2, rows), F32),
             pltpu.VMEM((NF // 2, NB, 128), F32),
             pltpu.VMEM((NF // 2, NB, 128), F32),
+            dma((3,)),
             dma((8,)),
             dma((NC,)),
             dma((NC,)),
@@ -518,10 +549,27 @@
             dma((NC,)),
             dma((NC,)),
         ],
-        compiler_params=pltpu.CompilerParams(collective_id=0, has_side_effects=True),
+        compiler_params=pltpu.CompilerParams(
+            collective_id=0, has_side_effects=True, vmem_limit_bytes=40 * 1024 * 1024
+        ),
         name="spod",
-    )(snapshots, weight.reshape(-1, 128), start_vec.transpose(1, 2, 0), table)
-    return gram.reshape(per, 2, NB, NB), modes.reshape(per, 2, NC * rows)
+    )(
+        *(
+            pltpu.with_memory_space_constraint(a, pltpu.HBM)
+            for a in (snapshots, weight.reshape(-1, 128), start_vec.transpose(1, 2, 0), jnp.asarray(table))
+        )
+    )
+    return pl.pallas_call(
+        finish,
+        out_shape=(
+            jax.ShapeDtypeStruct((per, 2, NB, NB), F32),
+            jax.ShapeDtypeStruct((per, 2, NC * rows), F32),
+        ),
+        in_specs=[vmem, vmem],
+        out_specs=(vmem, vmem),
+        compiler_params=pltpu.CompilerParams(vmem_limit_bytes=16 * 1024 * 1024),
+        name="finish",
+    )(gram, modes)
 
 
 def solution(mesh):

time: 46.9 us -> 43.3 us (0.923)
  local copies, waits for them, and re-layouts: 3.38 us -> 0 us
    reshape x1 -> x0, local copies, waits for them, and re-layouts: 1.71 us -> none  [shards(): return (gram.reshape(per, 2, NB, NB), modes.reshape(per, 2, NC * rows))]
    unnamed x1 -> x0, local copies, waits for them, and re-layouts: 1.67 us -> none
    pallas_call x1, Pallas kernels: 42.7 us -> 41.6 us  [shards(): pl.pallas_call(functools.partial(kernel, nz, total_rows), out_shape=(jax....]
    pallas_call x0 -> x1, Pallas kernels: none -> 0.89 us  [shards(): pl.pallas_call(finish, out_shape=(jax.ShapeDtypeStruct((per, 2, NB, NB),...]
where the time goes in v3:
time: 43.3 us; the launch traced here: 43.2 us
  Pallas kernels  42.5 us (98%)
  between operations  0.64 us (1%)
    pallas_call x1, Pallas kernels, shards(): pl.pallas_call(functools.partial(kernel, nz, total_rows), out_shape=(jax....  41.6 us
    pallas_call x1, Pallas kernels, shards(): pl.pallas_call(finish, out_shape=(jax.ShapeDtypeStruct((per, 2, NB, NB),...  0.89 us

profile of v3, /device:TPU:1, one launch (start us, length us, event | category | flops | bytes accessed | tf_op | source)
XLA Modules:
  0.0 43.2 jit_solution(7300034792575528686)
XLA Ops:
  0.6 41.6 %spod.1 = (f32[64,128]{1,0:T(8,128)S(1)}, f32[8,16,384]{2,1,0:T(8,128)S(1)}) custom-call(f32[2112,384]{1,0:T(8,128)} %snap_hbm.1, f32[24,128]{1,0:T(8,128)} %bitcast.3, f32[2,32,64]{2,1,0:T(8,128)} %bitcast.2, bf16[256,256]{1,0:T(8,128)(2,1)} %constant.2.clone.table_hbm), custom_call_target="tpu_custom_call" | custom-call | tf_op jit(solution)/shard_map/spod/pallas_call | solution.py:499
  42.3 0.9 %finish.1 = (f32[8,2,32,32]{3,2,1,0:T(8,128)}, f32[8,2,3072]{2,1,0:T(2,128)}) custom-call(f32[64,128]{1,0:T(8,128)S(1)} %get-tuple-element.4.gram_ref, f32[8,16,384]{2,1,0:T(8,128)S(1)} %get-tuple-element.5.modes_ref), custom_call_target="tpu_custom_call" | custom-call | tf_op jit(solution)/shard_map/finish/pallas_call | solution.py:562

commit v4 on v3

--- a/solution.py
+++ b/solution.py
@@ -34,6 +34,10 @@
     top = np.concatenate([high[:, :HALF], high[:, :HALF], high[:, HALF:], high[:, HALF:]], axis=1)
     bottom = np.concatenate([low[:, :HALF], zero, low[:, HALF:], zero], axis=1)
     return np.concatenate([top, bottom], axis=0)
+
+
+def far(n):
+    return sorted(range(1, n), key=lambda d: -min(d, n - d))
 
 
 def split(value):
@@ -141,11 +145,11 @@
     barrier = pltpu.get_barrier_semaphore()
     for i in range(NC - 1):
         pl.semaphore_signal(barrier, inc=1, device_id={"freq": freq_peer(i)}, device_id_type=MESH)
-    for d in range(1, NY):
+    for d in far(NY):
         pl.semaphore_signal(
             barrier, inc=1, device_id={"pts": zc * NY + (yc + d) % NY}, device_id_type=MESH
         )
-    for d in range(1, nz):
+    for d in far(nz):
         pl.semaphore_signal(
             barrier, inc=1, device_id={"pts": (zc + d) % nz * NY + yc}, device_id_type=MESH
         )
@@ -168,10 +172,9 @@
                 jnp.broadcast_to(coeffs[:, n : n + 1], (NB, 128))
                 for n in (4 * i + 2 * odd, 4 * i + 2 * odd + 1, NF + 4 * i + 2 * odd, NF + 4 * i + 2 * odd + 1)
             )
-            at = seg if odd == 0 else (seg + 2) % 4
             pair = 2 * i + odd
-            sa_ref[pair] = jnp.where(at == 0, r1, jnp.where(at == 1, r2, jnp.where(at == 2, i1, i2)))
-            sb_ref[pair] = jnp.where(at == 0, i1, jnp.where(at == 1, i2, jnp.where(at == 2, -r1, -r2)))
+            sa_ref[pair] = jnp.where(seg == 0, r1, jnp.where(seg == 1, i1, jnp.where(seg == 2, r2, i2)))
+            sb_ref[pair] = jnp.where(seg == 0, i1, jnp.where(seg == 1, -r1, jnp.where(seg == 2, i2, -r2)))
 
     total = jnp.zeros((24, rows), F32)
     for i in range(chunks):
@@ -202,7 +205,6 @@
                 at = m * rows + j * 128
                 q_ref[j, pl.ds(b + m, 2 * NF, stride=PITCH), :] = value[:, at : at + 128]
 
-    pl.semaphore_wait(barrier, NC - 1 + NY - 1 + nz - 1)
 
     per = NF // NC
     block = per * 2 * NB
@@ -231,59 +233,61 @@
     lane4 = lanes((per // 2, 128))
     lane = lanes((NB, 128))
 
-    def split_of(owner, p):
-        first = pl.multiple_of(owner * block + p * 128, 128)
-        hs, ls = [], []
+    order = [freq_peer(i) for i in range(NC - 1)] + [me]
+
+    def split_of(slot, p):
         for n in range(4):
-            source = (owner * (2 * per) + p * 4 + n) * PITCH
+            source = (order[slot] * (2 * per) + p * 4 + n) * PITCH
             value = [q_ref[j, pl.ds(source, NB), :] for j in range(groups)]
             high, low = split(jnp.concatenate(value, axis=1))
-            ah_ref[pl.ds(first + n * NB, NB), :] = high
-            al_ref[pl.ds(first + n * NB, NB), :] = low
-            hs.append(high); ls.append(low)
-        return hs, ls
-
-    def operands(hs, ls, p):
-        rh, ih = jnp.concatenate([hs[0], hs[2]], axis=0), jnp.concatenate([hs[1], hs[3]], axis=0)
-        rl, il = jnp.concatenate([ls[0], ls[2]], axis=0), jnp.concatenate([ls[1], ls[3]], axis=0)
-        h1 = jnp.concatenate([rh, ih], axis=1)
-        l1 = jnp.concatenate([rl, il], axis=1)
-        h2 = jnp.concatenate([ih, -rh], axis=1)
-        l2 = jnp.concatenate([il, -rl], axis=1)
-        right = [h1, h2, l1, l2] if p % 2 == 0 else [h2, h1, l2, l1]
-        return jnp.concatenate([h1, l1], axis=0), jnp.concatenate(right, axis=0)
-
-    def gram_of(owner):
+            at = slot * block + p * 128 + n * NB
+            ah_ref[at : at + NB, :] = high
+            al_ref[at : at + NB, :] = low
+
+    def pair_gram(slot, p):
+        at = slot * block + p * 128
+        high = ah_ref[at : at + 128, :]
+        out = dot_t(high, jnp.concatenate([high, al_ref[at : at + 128, :]], axis=0))
+        cross = out[:, 128:]
+        z = out[:, :128] + (cross + cross.T)
+        r1, i1, r2, i2 = (z[n * NB : (n + 1) * NB] for n in range(4))
+        even = jnp.where(lane < 64, r1, r2)
+        odd = jnp.where(lane < 64, i1, i2)
+        return jnp.where(
+            seg % 2 == 0, even + pltpu.roll(odd, 96, 1), even - pltpu.roll(odd, 32, 1)
+        )
+
+    def gram_of(slot):
+        owner = order[slot]
         parts_a, parts_b, packed = [], [], None
         for p in range(per // 2):
-            left, right = operands(*split_of(owner, p), p)
-            out = dot_t(left, right)
-            z = out[0:64, 0:128] + (out[0:64, 128:256] + out[64:128, 0:128])
-            g = jnp.where(seg % 2 == 0, z[0:32], z[32:64])
+            g = pair_gram(slot, p)
+            if slot + 1 < NC:
+                split_of(slot + 1, p)
             pair = owner * (per // 2) + p
             parts_a.append(jnp.sum(g * sa_ref[pair], axis=0, keepdims=True))
             parts_b.append(jnp.sum(g * sb_ref[pair], axis=0, keepdims=True))
-            half = jnp.where(upper, g, pltpu.roll(g, 64, 1))
             if p % 2 == 0:
-                packed = half
+                packed = jnp.where(upper, g, pltpu.roll(g, 96, 1))
             else:
-                both = jnp.where(lane < 64, packed, half)
+                half = jnp.where(upper, pltpu.roll(g, 32, 1), g)
+                both = jnp.where(seg % 2 == 0, packed, half)
                 gs_ref[owner, pl.ds(p // 2 * NB, NB), :] = both
         va = jnp.concatenate(parts_a, axis=0)
         vb = jnp.concatenate(parts_b, axis=0)
         vs_ref[owner] = jnp.where(
-            lane4 < 64, va + pltpu.roll(va, 64, 1), vb + pltpu.roll(vb, 64, 1)
-        )
-
-    def gram_step(i):
-        owner = freq_peer(i)
-        gram_of(owner)
-        vx_copy(owner, me).start()
-        gram_copy(owner, me).start()
-
-    for i in range(NC - 1):
-        gram_step(i)
-    gram_of(me)
+            lane4 // 32 % 2 == 0, va + pltpu.roll(va, 96, 1), vb + pltpu.roll(vb, 32, 1)
+        )
+
+    for p in range(per // 2):
+        split_of(0, p)
+    for slot in range(NC):
+        gram_of(slot)
+        if slot == 0:
+            pl.semaphore_wait(barrier, NC - 1 + NY - 1 + nz - 1)
+        if slot < NC - 1:
+            vx_copy(order[slot], me).start()
+            gram_copy(order[slot], me).start()
     vx_ref[me] = vs_ref[me]
     gr_ref[me] = gs_ref[me]
 
@@ -326,7 +330,7 @@
             device_id_type=MESH,
         )
 
-    for d in range(1, NY):
+    for d in far(NY):
         other = (yc + d) % NY
         spread(vy_ref, vy_s, vy_r, yc, other, y_dev(other)).start()
 
@@ -345,75 +349,66 @@
             device_id_type=MESH,
         )
 
-    for d in range(1, NY):
+    for d in far(NY):
         gram_y((yc + d) % NY, yc).start()
     gy_ref[yc] = gx_ref[pl.ds(pl.multiple_of(yc * gsub, gsub), gsub), :]
 
-    for d in range(1, NY):
+    for d in far(NY):
         other = (yc + d) % NY
         arrival(vy_ref, vy_s, vy_r, other, y_dev(other)).wait_recv()
     vz_ref[zc] = total_of(vy_ref, NY)
-    for d in range(1, nz):
+    for d in far(nz):
         other = (zc + d) % nz
         spread(vz_ref, vz_s, vz_r, zc, other, z_dev(other)).start()
 
-    for d in range(1, NY):
+    for d in far(NY):
         other = (yc + d) % NY
         gram_y(other, other).wait_recv()
     gz_ref[zc] = total_of(gy_ref, NY)
-    for d in range(1, nz):
+    for d in far(nz):
         other = (zc + d) % nz
         spread(gz_ref, gz_s, gz_r, zc, other, z_dev(other)).start()
 
-    for d in range(1, nz):
+    for d in far(nz):
         other = (zc + d) % nz
         arrival(vz_ref, vz_s, vz_r, other, z_dev(other)).wait_recv()
     v = total_of(vz_ref, nz) * (1.0 / total_rows)
 
-    odd = (lane4 // 32) % 2 == 1
-    turned = pltpu.roll(v, 64, 1)
-    vr = jnp.where(lane4 < 64, v, turned)
-    vi = jnp.where(lane4 < 64, turned, v)
     square = v * v
-    square = square + pltpu.roll(square, 64, 1)
-    norm1 = jnp.sum(jnp.where(lane4 < 32, square, 0.0), axis=1, keepdims=True) * (1.0 / NB)
-    norm2 = jnp.sum(jnp.where((lane4 >= 32) & (lane4 < 64), square, 0.0), axis=1, keepdims=True)
-    norm2 = norm2 * (1.0 / NB)
-    scale = jnp.where(odd, 1.0 / jnp.sqrt(norm2 + 1e-06), 1.0 / jnp.sqrt(norm1 + 1e-06))
-    yr = vr * scale
-    yi = vi * scale
-    k1re = jnp.where(odd, -pltpu.roll(yi, 32, 1), yr)
-    k1im = jnp.where(odd, pltpu.roll(yr, 32, 1), yi)
-    k2re = jnp.where(odd, -yi, pltpu.roll(yr, 96, 1))
-    k2im = jnp.where(odd, yr, pltpu.roll(yi, 96, 1))
-    pieces = []
-    for p in range(per // 2):
-        pieces += [w[p : p + 1] for w in (k1re, k1im, k2re, k2im)]
-    e_ref[me] = jnp.concatenate(pieces, axis=0)
+    norm1 = jnp.sum(jnp.where(lane4 < 64, square, 0.0), axis=1, keepdims=True) * (1.0 / NB)
+    norm2 = jnp.sum(jnp.where(lane4 >= 64, square, 0.0), axis=1, keepdims=True) * (1.0 / NB)
+    y = v * (1.0 / jnp.sqrt(jnp.where(lane4 < 64, norm1, norm2) + 1e-06))
+    turned = pltpu.roll(y, 64, 1)
+    e_ref[me] = jnp.concatenate(
+        [jnp.where(lane4 < 64, y, turned), jnp.where(lane4 < 64, turned, y)], axis=0
+    )
 
     for i in range(NC - 1):
         to = freq_peer(i)
         spread(e_ref, e_s, e_r, me, to, {"freq": to}).start()
 
-    own = lanes((2 * per, block)) // 64 == lanes((2 * per, block), 0) // 2
-
-    def project(owner):
-        e = e_ref[owner]
+    line = lanes((2 * per, block), 0)
+    own = lanes((2 * per, block)) // 64 == line % (per // 2) * 2 + line % per // (per // 2)
+    sign = jnp.where(lanes((per, 128)) // 32 % 2 == 0, 1.0, -1.0)
+
+    def project(slot):
+        y = e_ref[order[slot]]
+        e = jnp.concatenate([y * sign, pltpu.roll(y, 32, 1)], axis=0)
         left = jnp.where(own, jnp.concatenate([e] * (block // 128), axis=1), 0.0)
         high, low = split(left)
-        first = pl.multiple_of(owner * block, block)
-        right = ah_ref[pl.ds(first, block), :]
+        first = slot * block
+        right = ah_ref[first : first + block, :]
         both = dot(jnp.concatenate([high, low], axis=0), right)
-        out = both[: 2 * per] + both[2 * per :] + dot(high, al_ref[pl.ds(first, block), :])
+        out = both[: 2 * per] + both[2 * per :] + dot(high, al_ref[first : first + block, :])
         return out * inv_root
 
-    mr_ref[me] = project(me)
-
-    for d in range(1, nz):
+    mr_ref[me] = project(NC - 1)
+
+    for d in far(nz):
         other = (zc + d) % nz
         arrival(gz_ref, gz_s, gz_r, other, z_dev(other)).wait_recv()
     gf_ref[yc] = total_of(gz_ref, nz) * (1.0 / total_rows)
-    for d in range(1, NY):
+    for d in far(NY):
         other = (yc + d) % NY
         spread(gf_ref, ga_s, ga_r, yc, other, y_dev(other)).start()
 
@@ -431,13 +426,13 @@
         owners = [freq_peer(i) for i in step]
         for owner in owners:
             arrival(e_ref, e_s, e_r, owner, {"freq": owner}).wait_recv()
-        values = [project(owner) for owner in owners]
+        values = [project(i) for i in step]
         for owner, value in zip(owners, values):
             ms_ref[owner] = value
         for owner in owners:
             modes_copy(owner, me).start()
 
-    for d in range(1, NY):
+    for d in far(NY):
         other = (yc + d) % NY
         arrival(gf_ref, ga_s, ga_r, other, y_dev(other)).wait_recv()
     for i in range(NY):
@@ -448,12 +443,12 @@
         gram_copy(to, me).wait_send()
         vx_copy(to, me).wait_send()
         spread(e_ref, e_s, e_r, me, to, {"freq": to}).wait_send()
-    for d in range(1, NY):
+    for d in far(NY):
         other = (yc + d) % NY
         spread(vy_ref, vy_s, vy_r, yc, other, y_dev(other)).wait_send()
         gram_y(other, yc).wait_send()
         spread(gf_ref, ga_s, ga_r, yc, other, y_dev(other)).wait_send()
-    for d in range(1, nz):
+    for d in far(nz):
         other = (zc + d) % nz
         spread(vz_ref, vz_s, vz_r, zc, other, z_dev(other)).wait_send()
         spread(gz_ref, gz_s, gz_r, zc, other, z_dev(other)).wait_send()
@@ -473,7 +468,9 @@
     for s in range(NC):
         value = modes_ref[s]
         for k in range(per):
-            modes_out[k, :, s * rows : (s + 1) * rows] = value[2 * k : 2 * k + 2]
+            for c in range(2):
+                line = c * per + k % 2 * (per // 2) + k // 2
+                modes_out[k, c : c + 1, s * rows : (s + 1) * rows] = value[line : line + 1]
     packed = gram_ref[...]
     flipped = jnp.concatenate([packed, packed], axis=0).T
     above = lanes((NB, NB), 0) <= lanes((NB, NB))
@@ -485,8 +482,9 @@
             here = here if k == 0 else pltpu.roll(here, 128 - 32 * k, 1)
             there = there if q == 0 else pltpu.roll(there, 128 - 32 * q, 1)
             here, there = here[:, :NB], there[:, :NB]
-            gram_out[4 * q + k, 0] = jnp.where(above, here, there)
-            gram_out[4 * q + k, 1] = jnp.where(same, 0.0, jnp.where(above, -there, here))
+            freq = 4 * q + (0, 2, 1, 3)[k]
+            gram_out[freq, 0] = jnp.where(above, here, there)
+            gram_out[freq, 1] = jnp.where(same, 0.0, jnp.where(above, -there, here))
 
 
 def shards(nz, table, snapshots, weight, start_vec):
@@ -523,7 +521,7 @@
             pltpu.VMEM((NY, gram_rows // NY, 128), F32),
             pltpu.VMEM((NY, per // 2, 128), F32),
             pltpu.VMEM((nz, per // 2, 128), F32),
-            pltpu.VMEM((NC, per * 2, 128), F32),
+            pltpu.VMEM((NC, per, 128), F32),
             pltpu.VMEM((NC, per * 2, rows), F32),
             pltpu.VMEM((NC, per * 2, rows), F32),
             pltpu.VMEM((NF // 2, NB, 128), F32),

time: 43.3 us -> 42.8 us (0.988)
  Pallas kernels: 42.5 us -> 42 us
    pallas_call x1, Pallas kernels: 41.6 us -> 41.1 us  [shards(): pl.pallas_call(functools.partial(kernel, nz, total_rows), out_shape=(jax....]
where the time goes in v4:
time: 42.8 us; the launch traced here: 42.7 us
  Pallas kernels  42 us (98%)
  between operations  0.64 us (1%)
    pallas_call x1, Pallas kernels, shards(): pl.pallas_call(functools.partial(kernel, nz, total_rows), out_shape=(jax....  41.1 us
    pallas_call x1, Pallas kernels, shards(): pl.pallas_call(finish, out_shape=(jax.ShapeDtypeStruct((per, 2, NB, NB),...  0.92 us

profile of v4, /device:TPU:1, one launch (start us, length us, event | category | flops | bytes accessed | tf_op | source)
XLA Modules:
  0.0 42.7 jit_solution(8017564914411220872)
XLA Ops:
  0.6 41.1 %spod.1 = (f32[64,128]{1,0:T(8,128)S(1)}, f32[8,16,384]{2,1,0:T(8,128)S(1)}) custom-call(f32[2112,384]{1,0:T(8,128)} %snap_hbm.1, f32[24,128]{1,0:T(8,128)} %bitcast.3, f32[2,32,64]{2,1,0:T(8,128)} %bitcast.2, bf16[256,256]{1,0:T(8,128)(2,1)} %constant.2.clone.table_hbm), custom_call_target="tpu_custom_call" | custom-call | tf_op jit(solution)/shard_map/spod/pallas_call | solution.py:497
  41.7 0.9 %finish.1 = (f32[8,2,32,32]{3,2,1,0:T(8,128)}, f32[8,2,3072]{2,1,0:T(2,128)}) custom-call(f32[64,128]{1,0:T(8,128)S(1)} %get-tuple-element.4.gram_ref, f32[8,16,384]{2,1,0:T(8,128)S(1)} %get-tuple-element.5.modes_ref), custom_call_target="tpu_custom_call" | custom-call | tf_op jit(solution)/shard_map/finish/pallas_call | solution.py:560

commit v5 on v4

--- a/solution.py
+++ b/solution.py
@@ -28,12 +28,13 @@
     window = window / np.sqrt(np.sum(window * window))
     rows = np.stack([np.cos(phases) * window, -np.sin(phases) * window], axis=1)
     rows = rows.reshape(2 * NF, NFFT).astype(np.float32)
+    steady = [float(np.sum(rows[n], dtype=np.float64)) for n in (0, 2)]
     high = rows.astype(BF)
     low = (rows - high.astype(np.float32)).astype(BF)
     zero = np.zeros_like(low[:, :HALF])
     top = np.concatenate([high[:, :HALF], high[:, :HALF], high[:, HALF:], high[:, HALF:]], axis=1)
     bottom = np.concatenate([low[:, :HALF], zero, low[:, HALF:], zero], axis=1)
-    return np.concatenate([top, bottom], axis=0)
+    return np.concatenate([top, bottom], axis=0), steady
 
 
 def far(n):
@@ -60,6 +61,7 @@
 def kernel(
     nz,
     total_rows,
+    steady,
     snap_hbm,
     weight_hbm,
     start_hbm,
@@ -119,11 +121,10 @@
     xc = me // 2
     core = me % 2
 
-    chunks = load_sem.shape[0]
-    span = x_ref.shape[0] // chunks
+    bounds = [0, 17, halves]
 
     def load(i):
-        part = pl.ds(i * span, span)
+        part = pl.ds(bounds[i] * HALF, (bounds[i + 1] - bounds[i]) * HALF)
         return pltpu.make_async_copy(snap_hbm.at[part, :], x_ref.at[part, :], load_sem.at[i])
 
     small = [
@@ -134,9 +135,10 @@
     ]
     for copy in small[:2]:
         copy.start()
-    for i in range(chunks):
+    load(0).start()
+    small[2].start()
+    for i in range(1, len(bounds) - 1):
         load(i).start()
-    small[2].start()
 
     def freq_peer(i):
         step = (2, 1, 3, 0)[i // 2]
@@ -166,7 +168,7 @@
     seg = lanes((NB, 128)) // 32
     coeffs = jnp.concatenate([start_ref[0], start_ref[1]], axis=1)
 
-    for i in range(NF // 4):
+    def coefficient_tables(i):
         for odd in range(2):
             r1, r2, i1, i2 = (
                 jnp.broadcast_to(coeffs[:, n : n + 1], (NB, 128))
@@ -176,35 +178,54 @@
             sa_ref[pair] = jnp.where(seg == 0, r1, jnp.where(seg == 1, i1, jnp.where(seg == 2, r2, i2)))
             sb_ref[pair] = jnp.where(seg == 0, i1, jnp.where(seg == 1, -r1, jnp.where(seg == 2, i2, -r2)))
 
-    total = jnp.zeros((24, rows), F32)
-    for i in range(chunks):
-        load(i).wait()
-        for j in range(span // 24):
-            total = total + x_ref[i * span + j * 24 : i * span + (j + 1) * 24, :]
-    mean = jnp.sum(total, axis=0, keepdims=True) * (1.0 / x_ref.shape[0])
-
-    small[2].wait()
+    def sum_of(first, last):
+        out = x_ref[first * HALF : first * HALF + 32, :]
+        for n in range(first * HALF + 32, last * HALF, 32):
+            out = out + x_ref[n : n + 32, :]
+        return out
+
+    for i in range(12):
+        coefficient_tables(i)
+
+    load(0).wait()
+    total = sum_of(0, bounds[1])
+    about = jnp.sum(total, axis=0, keepdims=True) * (1.0 / (bounds[1] * HALF))
 
     def centre(j):
-        high, low = split((x_ref[j * HALF : (j + 1) * HALF, :] - mean) * root)
+        high, low = split((x_ref[j * HALF : (j + 1) * HALF, :] - about) * root)
         xc_ref[j * NFFT : j * NFFT + HALF, :] = high
         xc_ref[j * NFFT + HALF : (j + 1) * NFFT, :] = low
 
+    small[2].wait()
     done = 0
-    for b in range(0, NB, 2):
-        while done < min(b + 3 + 2, halves):
-            centre(done)
-            done += 1
-        right = jnp.concatenate(
-            [xc_ref[n * NFFT : (n + 2) * NFFT, :] for n in (b, b + 1)], axis=1
-        )
-        both = dot(table_ref[...], right)
-        value = both[: 2 * NF] + both[2 * NF :]
-        for m in range(2):
-            for j in range(groups):
-                at = m * rows + j * 128
-                q_ref[j, pl.ds(b + m, 2 * NF, stride=PITCH), :] = value[:, at : at + 128]
-
+    for chunk in range(len(bounds) - 1):
+        if chunk:
+            load(chunk).wait()
+        for b in range(max(bounds[chunk] - 1, 0), bounds[chunk + 1] - 1, 2):
+            while done < min(b + 5, bounds[chunk + 1]):
+                centre(done)
+                done += 1
+            right = jnp.concatenate(
+                [xc_ref[n * NFFT : (n + 2) * NFFT, :] for n in (b, b + 1)], axis=1
+            )
+            both = dot(table_ref[...], right)
+            value = both[: 2 * NF] + both[2 * NF :]
+            for m in range(2):
+                for j in range(groups):
+                    at = m * rows + j * 128
+                    q_ref[j, pl.ds(b + m, 2 * NF, stride=PITCH), :] = value[:, at : at + 128]
+        if chunk:
+            total = total + sum_of(bounds[chunk], bounds[chunk + 1])
+        if chunk == 1:
+            for i in range(12, NF // 4):
+                coefficient_tables(i)
+
+    mean = jnp.sum(total, axis=0, keepdims=True) * (1.0 / x_ref.shape[0])
+    shift = (mean - about) * root
+    for k, constant in enumerate(steady):
+        at = 2 * k * PITCH
+        for j in range(groups):
+            q_ref[j, at : at + NB, :] -= constant * shift[:, j * 128 : (j + 1) * 128]
 
     per = NF // NC
     block = per * 2 * NB
@@ -487,15 +508,16 @@
             gram_out[freq, 1] = jnp.where(same, 0.0, jnp.where(above, -there, here))
 
 
-def shards(nz, table, snapshots, weight, start_vec):
+def shards(nz, tables, snapshots, weight, start_vec):
     times, rows = snapshots.shape
+    table, steady = tables
     total_rows = weight.shape[0] * lax.axis_size("pts")
     per = NF // NC
     dma = pltpu.SemaphoreType.DMA
     vmem = pl.BlockSpec(memory_space=pltpu.VMEM)
     gram_rows = per // 4 * NB
     gram, modes = pl.pallas_call(
-        functools.partial(kernel, nz, total_rows),
+        functools.partial(kernel, nz, total_rows, steady),
         out_shape=(
             jax.ShapeDtypeStruct((gram_rows, 128), F32),
             jax.ShapeDtypeStruct((NC, per * 2, rows), F32),
@@ -527,7 +549,7 @@
             pltpu.VMEM((NF // 2, NB, 128), F32),
             pltpu.VMEM((NF // 2, NB, 128), F32),
             dma((3,)),
-            dma((8,)),
+            dma((2,)),
             dma((NC,)),
             dma((NC,)),
             dma((NY,)),

time: 42.8 us -> 42 us (0.981)
  Pallas kernels: 42 us -> 41.3 us
    pallas_call x1, Pallas kernels: 41.1 us -> 40.3 us  [shards(): pl.pallas_call(functools.partial(kernel, nz, total_rows, steady), out_sha...]
where the time goes in v5:
time: 42 us; the launch traced here: 41.9 us
  Pallas kernels  41.3 us (98%)
  between operations  0.64 us (2%)
    pallas_call x1, Pallas kernels, shards(): pl.pallas_call(functools.partial(kernel, nz, total_rows, steady), out_sha...  40.3 us
    pallas_call x1, Pallas kernels, shards(): pl.pallas_call(finish, out_shape=(jax.ShapeDtypeStruct((per, 2, NB, NB),...  0.92 us

profile of v5, /device:TPU:1, one launch (start us, length us, event | category | flops | bytes accessed | tf_op | source)
XLA Modules:
  0.0 41.9 jit_solution(1136478541398868817)
XLA Ops:
  0.6 40.3 %spod.1 = (f32[64,128]{1,0:T(8,128)S(1)}, f32[8,16,384]{2,1,0:T(8,128)S(1)}) custom-call(f32[2112,384]{1,0:T(8,128)} %snap_hbm.1, f32[24,128]{1,0:T(8,128)} %bitcast.3, f32[2,32,64]{2,1,0:T(8,128)} %bitcast.2, bf16[256,256]{1,0:T(8,128)(2,1)} %constant.2.clone.table_hbm), custom_call_target="tpu_custom_call" | custom-call | tf_op jit(solution)/shard_map/spod/pallas_call | solution.py:519
  41.0 0.9 %finish.1 = (f32[8,2,32,32]{3,2,1,0:T(8,128)}, f32[8,2,3072]{2,1,0:T(2,128)}) custom-call(f32[64,128]{1,0:T(8,128)S(1)} %get-tuple-element.4.gram_ref, f32[8,16,384]{2,1,0:T(8,128)S(1)} %get-tuple-element.5.modes_ref), custom_call_target="tpu_custom_call" | custom-call | tf_op jit(solution)/shard_map/finish/pallas_call | solution.py:582

commit v6 on v5

--- a/solution.py
+++ b/solution.py
@@ -88,7 +88,6 @@
     vz_ref,
     e_ref,
     ms_ref,
-    mr_ref,
     sa_ref,
     sb_ref,
     small_sem,
@@ -423,7 +422,7 @@
         out = both[: 2 * per] + both[2 * per :] + dot(high, al_ref[first : first + block, :])
         return out * inv_root
 
-    mr_ref[me] = project(NC - 1)
+    modes_out[me] = project(NC - 1)
 
     for d in far(nz):
         other = (zc + d) % nz
@@ -436,7 +435,7 @@
     def modes_copy(to, slot):
         return pltpu.make_async_remote_copy(
             src_ref=ms_ref.at[to],
-            dst_ref=mr_ref.at[slot],
+            dst_ref=modes_out.at[slot],
             send_sem=m_s.at[to],
             recv_sem=m_r.at[slot],
             device_id={"freq": to},
@@ -477,8 +476,6 @@
     for i in (6, 2, 3, 4, 5, 0, 1):
         sender = freq_peer(i)
         modes_copy(sender, sender).wait_recv()
-    for s in range(NC):
-        modes_out[s] = mr_ref[s]
     for i in range(NC - 1):
         modes_copy(freq_peer(i), me).wait_send()
 
@@ -545,7 +542,6 @@
             pltpu.VMEM((nz, per // 2, 128), F32),
             pltpu.VMEM((NC, per, 128), F32),
             pltpu.VMEM((NC, per * 2, rows), F32),
-            pltpu.VMEM((NC, per * 2, rows), F32),
             pltpu.VMEM((NF // 2, NB, 128), F32),
             pltpu.VMEM((NF // 2, NB, 128), F32),
             dma((3,)),

time: 42 us -> 42 us (level)
  no operation moved by 1% of the time
where the time goes in v6:
time: 42 us; the launch traced here: 41.9 us
  Pallas kernels  41.3 us (98%)
  between operations  0.64 us (2%)
    pallas_call x1, Pallas kernels, shards(): pl.pallas_call(functools.partial(kernel, nz, total_rows, steady), out_sha...  40.3 us
    pallas_call x1, Pallas kernels, shards(): pl.pallas_call(finish, out_shape=(jax.ShapeDtypeStruct((per, 2, NB, NB),...  0.92 us

profile of v6, /device:TPU:1, one launch (start us, length us, event | category | flops | bytes accessed | tf_op | source)
XLA Modules:
  0.0 41.9 jit_solution(8488346828058438350)
XLA Ops:
  0.6 40.3 %spod.1 = (f32[64,128]{1,0:T(8,128)S(1)}, f32[8,16,384]{2,1,0:T(8,128)S(1)}) custom-call(f32[2112,384]{1,0:T(8,128)} %snap_hbm.1, f32[24,128]{1,0:T(8,128)} %bitcast.3, f32[2,32,64]{2,1,0:T(8,128)} %bitcast.2, bf16[256,256]{1,0:T(8,128)(2,1)} %constant.2.clone.table_hbm), custom_call_target="tpu_custom_call" | custom-call | tf_op jit(solution)/shard_map/spod/pallas_call | solution.py:516
  41.0 0.9 %finish.1 = (f32[8,2,32,32]{3,2,1,0:T(8,128)}, f32[8,2,3072]{2,1,0:T(2,128)}) custom-call(f32[64,128]{1,0:T(8,128)S(1)} %get-tuple-element.4.gram_ref, f32[8,16,384]{2,1,0:T(8,128)S(1)} %get-tuple-element.5.modes_ref), custom_call_target="tpu_custom_call" | custom-call | tf_op jit(solution)/shard_map/finish/pallas_call | solution.py:578
